TPU v7x, 32 devices: a whole 2x2x4 slice. The times are simulated.
32 devices in a mesh: lat: 4 (over y, x), ord: 8 (over z, core).
Axes of the slice: x: 2, y: 2, z: 4, core: 2. Of those that a mesh axis runs over, the one named last changes fastest.
Arguments:
- heights: bfloat16 [512, 43200], P(('lat', 'ord')), may hold values from -1.5 to 1.5
- panels: bfloat16 [512, 5120, 128], P('lat', 'ord'), may hold values from -0.25 to 0.25
- ord_slot: int32 [5120], replicated, may hold values from 0 to 5119, each once
- cutoffs: int32 [5120], P('ord'), may hold values from 13360 to 21599
Outputs:
- gravity: float32 [512, 43200], P(('lat', 'ord'))
Inputs may be any that keep to these rules, and one draw needn't show every extreme that they name: `ord_slot`: a permutation of the order slots.
All inputs are finite; a program needn't handle non-finite values.
Results may differ from a plain program's by a relative error of at most 0.0039.
Values may be sent and summed in bfloat16 or wider, within the bound.
No kernel may reach another device: no remote copies, remote signals or barrier semaphores. Data moves between devices by JAX's collectives and lax.ppermute only.
A program may use at most 192 MiB of HBM per device.

v0:
```python
import math

import jax
import jax.numpy as jnp
from jax import lax
from jax.sharding import PartitionSpec as P

LON_SLOW = 180
LON_FAST = 240
ORDERS = 5120
DEG = 128
NMAX = 21600


def slow_tables(slow):
    index = jnp.arange(slow, dtype=jnp.int32)
    phase = index[:, None] * index[None, :] % slow
    angle = 2.0 * math.pi / slow * phase.astype(jnp.float32)
    return (jnp.cos(angle), jnp.sin(angle))


def twiddle_tables(slow, fast, blocks):
    total = slow * fast
    first = jnp.arange(slow, dtype=jnp.int32)[:, None, None]
    middle = jnp.arange(fast, dtype=jnp.int32)[None, :, None]
    last = jnp.arange(blocks, dtype=jnp.int32)[None, None, :]
    phase = (middle * first + slow * middle * last) % total
    angle = 2.0 * math.pi / total * phase.astype(jnp.float32)
    return (jnp.cos(angle), jnp.sin(angle))


def forward_spectra(values, slow, fast, orders):
    count = values.shape[0]
    grid = values.reshape(count, slow, fast)
    cosine, sine = slow_tables(slow)
    first_real = jnp.einsum("raj,ak->rkj", grid, cosine, precision=lax.Precision.HIGHEST)
    first_imag = -jnp.einsum("raj,ak->rkj", grid, sine, precision=lax.Precision.HIGHEST)
    blocks = orders // slow + 1
    twist_cos, twist_sin = twiddle_tables(slow, fast, blocks)
    joined = jnp.concatenate([first_real, first_imag], 2)
    table = jnp.concatenate(
        [jnp.concatenate([twist_cos, -twist_sin], 2), jnp.concatenate([twist_sin, twist_cos], 2)], 1
    )
    second = jnp.einsum("rkj,kjq->rkq", joined, table, precision=lax.Precision.HIGHEST)
    scale_in = 1.0 / math.sqrt(slow * fast)
    spec_real = (
        second[:, :, :blocks].transpose(0, 2, 1).reshape(count, blocks * slow)[:, 1 : orders + 1]
    )
    spec_imag = (
        second[:, :, blocks:].transpose(0, 2, 1).reshape(count, blocks * slow)[:, 1 : orders + 1]
    )
    return (spec_real * scale_in, spec_imag * scale_in)


def inverse_field(full_real, full_imag, slow, fast):
    count = full_real.shape[0]
    blocks = full_real.shape[1] // slow
    grid_real = full_real.reshape(count, blocks, slow).transpose(0, 2, 1)
    grid_imag = full_imag.reshape(count, blocks, slow).transpose(0, 2, 1)
    joined = jnp.concatenate([grid_real, grid_imag], 2)
    twist_cos, twist_sin = twiddle_tables(slow, fast, blocks)
    cos_turned = twist_cos.transpose(0, 2, 1)
    sin_turned = twist_sin.transpose(0, 2, 1)
    table = jnp.concatenate(
        [
            jnp.concatenate([cos_turned, sin_turned], 2),
            jnp.concatenate([-sin_turned, cos_turned], 2),
        ],
        1,
    )
    second = jnp.einsum("rkq,kqj->rkj", joined, table, precision=lax.Precision.HIGHEST)
    cosine, sine = slow_tables(slow)
    field = jnp.einsum("rkj,ka->raj", second[:, :, :fast], cosine, precision=lax.Precision.HIGHEST)
    field = field - jnp.einsum(
        "rkj,ka->raj", second[:, :, fast:], sine, precision=lax.Precision.HIGHEST
    )
    return field.reshape(count, slow * fast)


def fold_powers(terms, factors):
    slots = terms.shape[1]
    width = terms.shape[2]
    return jnp.sum(terms.reshape(3, 2, slots, width) * factors[:, None, None, :], axis=0)


def local(heights, panels, ord_slot, cutoffs):
    lat_count = lax.axis_size("lat")
    ord_count = lax.axis_size("ord")
    level = heights.astype(jnp.float32)
    cycle_dev = level.shape[0]
    square = level * level
    powers = jnp.concatenate([level, square, square * level], 0)
    spec_real, spec_imag = forward_spectra(powers, LON_SLOW, LON_FAST, ORDERS)
    picked = jnp.stack(
        [
            spec_real[:, ord_slot].reshape(3, cycle_dev, ORDERS),
            spec_imag[:, ord_slot].reshape(3, cycle_dev, ORDERS),
        ],
        1,
    )
    picked = picked.reshape(6, cycle_dev, ORDERS).astype(jnp.bfloat16)
    sums = jnp.einsum(
        "xrk,rkn->xkn",
        lax.all_to_all(picked, "ord", split_axis=2, concat_axis=1, tiled=True),
        panels,
        preferred_element_type=jnp.float32,
    )
    stride = (NMAX - ORDERS) // DEG
    degree_int = ORDERS + jnp.arange(DEG, dtype=jnp.int32) * stride
    degree = degree_int.astype(jnp.float32)
    factors = jnp.stack(
        [
            jnp.ones_like(degree),
            (degree + 2.0) / (2.0 * NMAX),
            (degree + 2.0) * (degree + 1.0) / (6.0 * NMAX * NMAX),
        ]
    )
    keep = (degree_int[None, :] <= cutoffs[:, None]).astype(jnp.float32)
    terms = fold_powers(sums, factors)
    total = lax.psum(terms, "lat")
    coeffs = (total * keep[None]).astype(jnp.bfloat16)
    synthesis = jnp.einsum("rkn,ckn->crk", panels, coeffs, preferred_element_type=jnp.float32)
    returned = lax.all_to_all(synthesis, "ord", split_axis=1, concat_axis=2, tiled=True)
    blocks = ORDERS // LON_SLOW + 1
    target = ord_slot + 1
    full_real = (
        jnp.zeros((cycle_dev, blocks * LON_SLOW), jnp.float32).at[:, target].set(returned[0])
    )
    full_imag = (
        jnp.zeros((cycle_dev, blocks * LON_SLOW), jnp.float32).at[:, target].set(returned[1])
    )
    field = inverse_field(full_real, full_imag, LON_SLOW, LON_FAST)
    cycles_all = cycle_dev * lat_count * ord_count
    return field * math.sqrt(cycles_all / (DEG * ORDERS))


def solution(mesh):
    return jax.shard_map(
        local,
        mesh=mesh,
        in_specs=(P(("lat", "ord"), None), P("lat", "ord", None), P(), P("ord")),
        out_specs=P(("lat", "ord"), None),
        check_vma=False,
    )
```

profile of v0, /device:TPU:1, one launch (start us, length us, event | category | flops | bytes accessed | tf_op | source)
XLA Modules:
  0.0 486.3 jit_solution(7475713609874748307)
XLA Ops:
  8.5 3.5 pad_maximum_fusion.1
  12.1 11.4 %reshape.129 = f32[48,180,240]{2,1,0:T(8,128)} reshape(f32[48,43200]{1,0:T(8,128)} %pad_maximum_fusion.1) | data formatting | bytes 16588800 | tf_op jit(solution)/shard_map/reshape | solution.py:34
  23.5 13.0 %convolution_bitcast_fusion = f32[48,180,240]{2,1,0:T(8,128)S(1)} fusion(f32[48,180,240]{2,1,0:T(8,128)} %reshape.129), kind=kOutput, calls=%fused_computation.48 | convolution fusion | flops 4479267840 | bytes 16588800 | tf_op jit(solution)/shard_map/raj,ak->rkj/dot_general | solution.py:36
  36.5 10.0 %negate_bitcast_fusion = f32[48,180,240]{2,1,0:T(8,128)S(1)} fusion(f32[48,180,240]{2,1,0:T(8,128)S(1)} %copy-done), kind=kOutput, calls=%fused_computation.26 | convolution fusion | flops 4481341440 | bytes 16588800 | tf_op jit(solution)/shard_map/raj,ak->rkj/dot_general | solution.py:37
  46.5 7.9 %pad_maximum_fusion = f32[48,180,480]{2,1,0:T(8,128)} fusion(f32[48,180,240]{2,1,0:T(8,128)S(1)} %negate_bitcast_fusion, f32[48,180,240]{2,1,0:T(8,128)S(1)} %convolution_bitcast_fusion), kind=kLoop, calls=%fused_computation.24 | loop fusion | flops 4147200 | bytes 33177600 | tf_op jit(solution)/shard_map/concatenate | solution.py:40
  54.4 26.4 %fusion.50 = (f32[180,240,29]{1,2,0:T(8,128)}, f32[180,240,29]{1,2,0:T(8,128)}, f32[180,240,29]{1,2,0:T(8,128)}) fusion(s32[240,29]{0,1:T(8,128)S(1)} %iota_multiply_fusion.1, s32[180,240]{1,0:T(8,128)S(1)} %iota_multiply_fusion), kind=kLoop, calls=%fused_computation.60 | loop fusion | flops 12528000 | bytes 15234240 | tf_op jit(solution)/shard_map/neg | solution.py:42
  80.8 38.7 %fusion.42 = f32[48,180,58]{2,0,1:T(8,128)S(1)} fusion(f32[48,180,480]{2,1,0:T(8,128)} %pad_maximum_fusion, f32[180,240,29]{1,2,0:T(8,128)} %get-tuple-element.15, f32[180,240,29]{1,2,0:T(8,128)} %get-tuple-element.14, f32[180,240,29]{1,2,0:T(8,128)} %get-tuple-element.13), kind=kOutput, calls=%fused_computation.57 | convolution fusion | flops 2901484800 | bytes 33626880 | tf_op jit(solution)/shard_map/rkj,kjq->rkq/dot_general | solution.py:44
  119.6 4.8 slice_bitcast_fusion.1
  124.4 4.4 copy.110
  130.5 2.1 slice_multiply_fusion.1
  132.6 15.1 %gather_fusion = bf16[5120,48]{1,0:T(8,128)(2,1)S(1)} fusion(bf16[48,5120]{0,1:T(8,128)(2,1)S(1)} %slice_multiply_fusion.1, s32[5120]{0:T(1024)S(1)} %get-tuple-element.19), kind=kCustom, calls=%fused_computation | custom fusion | bytes 1003520 | tf_op jit(solution)/shard_map/gather | solution.py:96
  148.3 4.4 copy.111
  156.5 15.1 %gather_fusion.1 = bf16[5120,48]{1,0:T(8,128)(2,1)S(1)} fusion(bf16[48,5120]{0,1:T(8,128)(2,1)S(1)} %slice_multiply_fusion, s32[5120]{0:T(1024)S(1)} %get-tuple-element.19), kind=kCustom, calls=%fused_computation.1 | custom fusion | bytes 1003520 | tf_op jit(solution)/shard_map/gather | solution.py:97
  172.4 8.2 %copy.90 = bf16[6,16,5120]{1,0,2:T(8,128)(2,1)} copy(bf16[6,16,5120]{2,1,0:T(8,128)(2,1)S(1)} %bitcast.72) | data formatting | bytes 1966080 | tf_op jit(solution)/shard_map/convert_element_type | solution.py:101
  180.6 11.5 %reshape.179 = bf16[8,2,30720]{2,1,0:T(2,128)(2,1)} reshape(bf16[5120,6,16]{2,1,0:T(8,128)(2,1)} %bitcast.69) | data formatting | bytes 1966080
  192.0 6.4 %all-to-all-start = ((bf16[8,2,30720]{2,1,0:T(2,128)(2,1)}), bf16[8,2,30720]{2,1,0:T(2,128)(2,1)S(1)}, u32[]{:S(2)}, u32[]{:S(2)}) async-start(bf16[8,2,30720]{2,1,0:T(2,128)(2,1)} %reshape.179), calls=%async_computation | async-start | bytes 1966080 | tf_op jit(solution)/shard_map/all_to_all | solution.py:104
  198.4 24.2 %all-to-all-done = bf16[8,2,30720]{2,1,0:T(2,128)(2,1)S(1)} async-done(((bf16[8,2,30720]{2,1,0:T(2,128)(2,1)}), bf16[8,2,30720]{2,1,0:T(2,128)(2,1)S(1)}, u32[]{:S(2)}, u32[]{:S(2)}) %all-to-all-start) | async-done | bytes 983072 | tf_op jit(solution)/shard_map/all_to_all | solution.py:104
  222.6 11.0 %reshape.180 = bf16[5120,6,16]{2,1,0:T(8,128)(2,1)} reshape(bf16[8,2,30720]{2,1,0:T(2,128)(2,1)S(1)} %all-to-all-done) | data formatting | bytes 1966080
  233.5 8.5 %copy.92 = bf16[6,8,16,640]{3,2,1,0:T(8,128)(2,1)S(1)} copy(bf16[6,8,16,640]{2,0,3,1:T(8,128)(2,1)} %bitcast.70) | data formatting | bytes 1966080 | tf_op jit(solution)/shard_map/all_to_all | solution.py:104
  243.4 26.1 %fusion.51 = f32[6,640,128]{2,0,1:T(8,128)S(1)} fusion(bf16[6,128,640]{1,0,2:T(8,128)(2,1)S(1)} %copy.93, bf16[128,640,128]{2,1,0:T(8,128)(2,1)} %param.5), kind=kOutput, calls=%fused_computation.61 | convolution fusion | flops 125829120 | bytes 23920640 | tf_op jit(solution)/shard_map/xrk,rkn->xkn/dot_general | solution.py:102
  271.0 45.9 %all-reduce.2.cloned.1.call-done = f32[2,640,128]{2,1,0:T(8,128)} async-done(((f32[2,640,128]{2,1,0:T(8,128)}), f32[2,640,128]{2,1,0:T(8,128)}) %all-reduce.2.cloned.1.call-update) | async-done | bytes 655376 | tf_op jit(solution)/shard_map/psum | solution.py:120
  318.1 50.4 %fusion.61 = f32[2,128,640]{1,0,2:T(2,128)S(1)} fusion(bf16[128,640,128]{2,1,0:T(8,128)(2,1)} %param.5, bf16[2,640,128]{2,1,0:T(8,128)(2,1)S(1)} %multiply_convert_fusion), kind=kOutput, calls=%fused_computation.73 | convolution fusion | flops 41943040 | bytes 21954560 | tf_op jit(solution)/shard_map/rkn,ckn->crk/dot_general | solution.py:122
  369.9 5.3 %all-to-all-start.1 = ((f32[2,128,640]{2,0,1:T(2,128)}), f32[2,128,640]{2,0,1:T(2,128)S(1)}, u32[]{:S(2)}, u32[]{:S(2)}) async-start(f32[2,128,640]{2,0,1:T(2,128)} %copy.98), calls=%async_computation.1 | async-start | bytes 1310720 | tf_op jit(solution)/shard_map/all_to_all | solution.py:123
  375.2 26.6 %fusion.31 = (f32[180,29,240]{2,1,0:T(8,128)}, f32[180,29,240]{2,1,0:T(8,128)}, f32[180,29,240]{2,1,0:T(8,128)}) fusion(s32[29,240]{1,0:T(8,128)S(1)} %iota_multiply_fusion.2, s32[180,240]{1,0:T(8,128)S(1)} %iota_multiply_fusion), kind=kLoop, calls=%fused_computation.42 | loop fusion | flops 12528000 | bytes 15234240 | tf_op jit(solution)/shard_map/sin | solution.py:29
  401.9 2.2 copy.101
  404.2 14.0 %scatter_custom_fusion = f32[16,5220]{0,1:T(8,128)S(1)} fusion(s32[5120]{0:T(1024)S(1)} %get-tuple-element.20, f32[5120,16]{1,0:T(8,128)} %copy.101, f32[]{:T(128)} %constant.52.clone.1), kind=kCustom, calls=%fused_computation.69 | custom fusion | bytes 334592 | tf_op jit(solution)/shard_map/scatter | solution.py:127
  421.7 2.2 copy.105
  423.9 14.0 %scatter_custom_fusion.1 = f32[16,5220]{0,1:T(8,128)S(1)} fusion(s32[5120]{0:T(1024)S(1)} %get-tuple-element.20, f32[5120,16]{1,0:T(8,128)} %copy.105, f32[]{:T(128)} %constant.52.clone.1), kind=kCustom, calls=%fused_computation.67 | custom fusion | bytes 334592 | tf_op jit(solution)/shard_map/scatter | solution.py:130
  441.4 24.1 %fusion.39 = f32[16,180,480]{2,0,1:T(8,128)S(1)} fusion(f32[180,29,240]{2,1,0:T(8,128)} %get-tuple-element.18, f32[180,29,240]{2,1,0:T(8,128)} %get-tuple-element.17, f32[180,29,240]{2,1,0:T(8,128)} %get-tuple-element.16, f32[16,180,29]{2,0,1:T(8,128)} %bitcast.80, f32[16,180,29]{2,0,1:T(8,128)} %bitcast.79), kind=kOutput, calls=%fused_computation.56 | convolution fusion | flops 977351040 | bytes 21231360 | tf_op jit(solution)/shard_map/rkq,kqj->rkj/dot_general | solution.py:71
  466.6 4.9 %fusion.35 = f32[180,16,240]{2,0,1:T(8,128)S(1)} fusion(f32[16,180,240]{2,0,1:T(8,128)S(1)} %get-tuple-element.6), kind=kOutput, calls=%fused_computation.49 | convolution fusion | flops 1493283584 | bytes 5529600 | tf_op jit(solution)/shard_map/rkj,ka->raj/dot_general | solution.py:74
  471.5 5.1 %multiply_bitcast_fusion = f32[16,180,240]{2,1,0:T(8,128)S(1)} fusion(f32[180,16,240]{2,0,1:T(8,128)S(1)} %fusion.35, f32[16,180,240]{2,0,1:T(8,128)S(1)} %get-tuple-element.5), kind=kOutput, calls=%fused_computation.53 | convolution fusion | flops 1494665984 | bytes 8294400 | tf_op jit(solution)/shard_map/rkj,ka->raj/dot_general | solution.py:73
  476.6 2.5 mul.334
  (46 shorter events, 22.3 us)
Async XLA Ops:
  6.5 1.8 copy-start.1
  23.5 13.0 %copy-start = (f32[48,180,240]{2,1,0:T(8,128)S(1)}, f32[48,180,240]{2,1,0:T(8,128)}, u32[]{:S(2)}) copy-start(f32[48,180,240]{2,1,0:T(8,128)} %reshape.129) | copy-start | bytes 24883204
  128.8 3.8 copy-start.2
  192.0 30.6 %all-to-all-start = ((bf16[8,2,30720]{2,1,0:T(2,128)(2,1)}), bf16[8,2,30720]{2,1,0:T(2,128)(2,1)S(1)}, u32[]{:S(2)}, u32[]{:S(2)}) async-start(bf16[8,2,30720]{2,1,0:T(2,128)(2,1)} %reshape.179), calls=%async_computation | async-start | bytes 1966080 | tf_op jit(solution)/shard_map/all_to_all | solution.py:104
  198.4 118.6 %all-reduce.2.cloned.1.call-start = ((), (), s32[]{:S(2)}) async-start(), calls=%async_computation.2 | async-start | bytes 1310720 | tf_op jit(solution)/shard_map/psum | solution.py:120
  269.4 1.4 copy-start.3
  369.9 32.0 %all-to-all-start.1 = ((f32[2,128,640]{2,0,1:T(2,128)}), f32[2,128,640]{2,0,1:T(2,128)S(1)}, u32[]{:S(2)}, u32[]{:S(2)}) async-start(f32[2,128,640]{2,0,1:T(2,128)} %copy.98), calls=%async_computation.1 | async-start | bytes 1310720 | tf_op jit(solution)/shard_map/all_to_all | solution.py:123
Sparse Core Ops, SparseCore 0:
  271.0 45.9 all-reduce.1
where the time goes:
time: 493 us; the launch traced here: 486 us
  matrix products  172 us (35%)
  local copies, waits for them, and re-layouts  145 us (29%)
  other arithmetic  73.1 us (15%)
  waiting for transfers between devices  70.1 us (14%)
  between operations  14 us (3%)
  starting transfers between devices  11.7 us (2%)
    dot_general x1, matrix products, local(): jnp.einsum('rkn,ckn->crk', panels, coeffs, preferred_element_type=jnp.flo...  50.4 us
    psum x1, waiting for transfers between devices, local(): total = lax.psum(terms, 'lat')  45.9 us
    dot_general x1, matrix products, forward_spectra(): jnp.einsum('rkj,kjq->rkq', joined, table, precision=lax.Precision.HIGHEST)  38.7 us
    scatter x4, local copies, waits for them, and re-layouts, local(): jnp.zeros((cycle_dev, blocks * LON_SLOW), jnp.float32).at[:, target]  29.5 us
    sin x1, other arithmetic, twiddle_tables(): return (jnp.cos(angle), jnp.sin(angle))  26.6 us
    neg x1, other arithmetic, forward_spectra(): -twist_sin  26.4 us
    dot_general x1, matrix products, local(): jnp.einsum('xrk,rkn->xkn', lax.all_to_all(picked, 'ord', split_axis=2, co...  26.1 us
    all_to_all x1, waiting for transfers between devices, local(): lax.all_to_all(picked, 'ord', split_axis=2, concat_axis=1, tiled=True)  24.2 us
  transfers between devices with their start and end apart: 3, of which 2 were waited for; matrix products, arithmetic and copies ran while one was open for 6% of the time, Pallas kernels for 0%

commit v1 on v0

v1 whole, which is shorter than its diff:
```python
import functools
import math

import jax
import jax.numpy as jnp
import ml_dtypes
import numpy as np
from jax import lax
from jax.experimental import pallas as pl
from jax.experimental.pallas import tpu as pltpu
from jax.sharding import PartitionSpec as P

SLOW = 180
FAST = 240
HALF = SLOW // 2 + 1
KPAD = 96
QPAD = 32
APAD = 184
FPITCH = 136
IPITCH = 200
BATCH = 5
LANES = 256
ORDERS = 5120
DEG = 128
NMAX = 21600
LON = SLOW * FAST
f32 = jnp.float32
bf16 = jnp.bfloat16


def halves(table):
    high = table.astype(ml_dtypes.bfloat16)
    return high, (table - high.astype(np.float64)).astype(ml_dtypes.bfloat16)


def split(x):
    high = x.astype(bf16)
    return high, (x - high.astype(f32)).astype(bf16)


def angles(total, phase):
    return 2.0 * np.pi / total * (phase % total).astype(np.float64)


@functools.lru_cache
def forward_tables():
    k = np.arange(HALF)[:, None]
    a = np.arange(SLOW)[None, :]
    first = np.zeros((2 * KPAD, SLOW))
    first[:HALF] = np.cos(angles(SLOW, k * a))
    first[KPAD : KPAD + HALF] = -np.sin(angles(SLOW, k * a))
    j = np.arange(FAST)[None, :]
    twist = np.zeros((2, KPAD, FAST), np.float32)
    twist[0, :HALF] = np.cos(angles(LON, k * j)) / math.sqrt(LON)
    twist[1, :HALF] = np.sin(angles(LON, k * j)) / math.sqrt(LON)
    q = np.arange(QPAD)[:, None]
    last = np.concatenate([np.cos(angles(FAST, q * j)), np.sin(angles(FAST, q * j))])
    return np.concatenate(halves(first)), twist, np.concatenate(halves(last))


@functools.lru_cache
def inverse_tables(scale):
    q = np.arange(QPAD)[:, None]
    j = np.arange(FAST)[None, :]
    first = np.zeros((QPAD, 2 * LANES))
    first[:, :FAST] = np.cos(angles(FAST, q * j))
    first[:, LANES : LANES + FAST] = np.sin(angles(FAST, q * j))
    k = np.arange(HALF)[:, None]
    twist = np.zeros((2, KPAD, LANES), np.float32)
    twist[0, :HALF, :FAST] = scale * np.cos(angles(LON, k * j))
    twist[1, :HALF, :FAST] = scale * np.sin(angles(LON, k * j))
    a = np.arange(SLOW)[:, None]
    last = np.zeros((APAD, 2 * KPAD))
    last[:SLOW, :HALF] = np.cos(angles(SLOW, a * k.T))
    last[:SLOW, KPAD : KPAD + HALF] = -np.sin(angles(SLOW, a * k.T))
    high, low = halves(first)
    return np.concatenate([high, high, low]), twist, np.concatenate(halves(last))


def swap_blocks(x):
    shape = (x.shape[0] // 8, 8, 128)
    x = x.reshape(shape)
    rows = lax.broadcasted_iota(jnp.int32, shape, 1)
    cols = lax.broadcasted_iota(jnp.int32, shape, 2) // 16
    for bit in (4, 2, 1):
        moved = pltpu.roll(pltpu.roll(x, 8 - bit, 1), 16 * bit, 2)
        if bit < 4:
            down = pltpu.roll(pltpu.roll(x, bit, 1), 128 - 16 * bit, 2)
            moved = jnp.where((rows & bit) == 0, moved, down)
        x = jnp.where((rows & bit) == (cols & bit), x, moved)
    return x.reshape(shape[0] * 8, 128)


def forward_kernel(
    per_chunk, chunks, addr_ref, x_ref, first_ref, twist_ref, last_ref, out_ref, ya, yb, z, g
):
    cycles = x_ref.shape[0]
    rest = FAST - 128

    def first_stage(r, carry):
        level = x_ref[r].astype(f32)
        square = level * level
        for p, value in enumerate((level, square, square * level)):
            high, low = split(value)
            o = jnp.dot(first_ref[...], high, preferred_element_type=f32)
            o = o[: 2 * KPAD] + o[2 * KPAD :]
            if p > 0:
                o = o + jnp.dot(first_ref[: 2 * KPAD], low, preferred_element_type=f32)
            real, imag = o[:KPAD], o[KPAD:]
            cosine, sine = twist_ref[0], twist_ref[1]
            turned = (real * cosine + imag * sine, imag * cosine - real * sine)
            for c in range(2):
                row = c * 64 + p * cycles + r
                ya[pl.ds(row, KPAD, stride=FPITCH), :] = turned[c][:, :128]
                yb[pl.ds(row, KPAD, stride=FPITCH), 0:rest] = turned[c][:, 128:]
        return carry

    lax.fori_loop(0, cycles, first_stage, 0)
    flip = jnp.where(lax.broadcasted_iota(jnp.int32, (QPAD, 128), 1) < 64, 1.0, -1.0)

    def second_stage(k, carry):
        base = pl.multiple_of(k * FPITCH, 8)
        value = jnp.concatenate([ya[pl.ds(base, 128), :], yb[pl.ds(base, 128), 0:rest]], 1)
        high, low = split(value)
        dims = (((1,), (1,)), ((), ()))
        o = lax.dot_general(last_ref[...], high, dims, preferred_element_type=f32)
        o = o[: 2 * QPAD] + o[2 * QPAD :]
        o = o + lax.dot_general(last_ref[: 2 * QPAD], low, dims, preferred_element_type=f32)
        oc = o[:QPAD]
        os = pltpu.roll(o[QPAD:], 64, 1)
        place = pl.multiple_of(k * 64, 64)
        z[pl.ds(place, QPAD), :] = oc + flip * os
        z[pl.ds(place + QPAD, QPAD), :] = flip * oc - os
        return carry

    lax.fori_loop(0, HALF, second_stage, 0, unroll=7)

    def pick(b, carry):
        for i in range(128 * BATCH):
            g[pl.ds(i, 1), :] = z[pl.ds(addr_ref[b * 128 * BATCH + i], 1), :]
        for n in range(BATCH):
            turned = g[128 * n : 128 * n + 128, :].T
            wanted = jnp.concatenate([turned[:48], turned[64:112]], 0)
            turned = swap_blocks(wanted)
            for u in range(8 // per_chunk):
                columns = []
                for h in range(2):
                    parts = []
                    for x in range(6):
                        row = (x % 2) * 48 + (x // 2) * 16 + h * 8 + u * per_chunk
                        parts.append(turned[row : row + per_chunk])
                    columns.append(jnp.concatenate(parts, 0))
                piece = (b * BATCH + n) * (8 // per_chunk) + u
                out_ref[piece // chunks, piece % chunks] = jnp.concatenate(columns, 1).astype(bf16)
        return carry

    lax.fori_loop(0, ORDERS // 128 // BATCH, pick, 0)


def forward(heights, addr, dests, slots):
    cycles = heights.shape[0]
    chunk = math.gcd(slots, 128)
    chunks, per_chunk = slots // chunk, chunk // 16
    first, twist, last = forward_tables()
    vmem = pl.BlockSpec(memory_space=pltpu.VMEM)
    return pl.pallas_call(
        functools.partial(forward_kernel, per_chunk, chunks),
        in_specs=[pl.BlockSpec(memory_space=pltpu.SMEM)] + [vmem] * 4,
        out_specs=vmem,
        out_shape=jax.ShapeDtypeStruct((dests, chunks, 6 * per_chunk, 16 * cycles), bf16),
        scratch_shapes=[
            pltpu.VMEM((KPAD * FPITCH, 128), f32),
            pltpu.VMEM((KPAD * FPITCH, 128), f32),
            pltpu.VMEM((KPAD * 64, 128), f32),
            pltpu.VMEM((128 * BATCH, 128), f32),
        ],
        name="forward",
    )(addr, heights.reshape(cycles, SLOW, FAST), first, twist, last)


def analysis_kernel(per_chunk, p_ref, panels_ref, q_ref, out_ref):
    sources = p_ref.shape[0]
    wide = p_ref.shape[3]
    span = sources * wide
    shape = (16, wide)
    mask = lax.broadcasted_iota(jnp.int32, shape, 1) % 16 == lax.broadcasted_iota(
        jnp.int32, shape, 0
    )
    owners = out_ref.shape[0]
    size = out_ref.shape[3]
    terms = [[], []]
    for kb in range(per_chunk):
        w = panels_ref[:, kb * 16 : (kb + 1) * 16, :].reshape(span, DEG)
        rows = []
        for x in range(6):
            row = x * per_chunk + kb
            cols = []
            for s in range(sources):
                line = jnp.broadcast_to(p_ref[s, 0, row : row + 1, :], shape)
                cols.append(jnp.where(mask, line, jnp.zeros((), bf16)))
            rows.append(jnp.concatenate(cols, 1))
        s = jnp.dot(jnp.concatenate(rows, 0), w, preferred_element_type=f32)
        for c in range(2):
            terms[c].append(
                q_ref[0:1] * s[16 * c : 16 * c + 16]
                + q_ref[1:2] * s[32 + 16 * c : 48 + 16 * c]
                + q_ref[2:3] * s[64 + 16 * c : 80 + 16 * c]
            )
    for c in range(2):
        total = jnp.concatenate(terms[c], 0)
        for owner in range(owners):
            out_ref[owner, 0, c] = total[owner * size : (owner + 1) * size].astype(out_ref.dtype)


def analysis(picked, panels, factors, owners):
    sources, chunks, rows, wide = picked.shape
    per_chunk = rows // 6
    chunk = per_chunk * 16
    size = chunk // owners
    return pl.pallas_call(
        functools.partial(analysis_kernel, per_chunk),
        grid=(chunks,),
        in_specs=[
            pl.BlockSpec((sources, 1, rows, wide), lambda i: (0, i, 0, 0)),
            pl.BlockSpec((panels.shape[0], chunk, DEG), lambda i: (0, i, 0)),
            pl.BlockSpec((8, DEG), lambda i: (0, 0)),
        ],
        out_specs=pl.BlockSpec((owners, 1, 2, size, DEG), lambda i: (0, i, 0, 0, 0)),
        out_shape=jax.ShapeDtypeStruct((owners, chunks, 2, size, DEG), bf16),
        name="analysis",
    )(picked, panels, factors)


def synthesis_kernel(per_chunk, me_ref, *refs):
    coeff_refs, panels_ref, out_ref = refs[:-2], refs[-2], refs[-1]
    dests = out_ref.shape[0]
    wide = out_ref.shape[3]
    span = dests * wide
    owners = len(coeff_refs)
    mask = lax.broadcasted_iota(jnp.int32, (16, span), 1) % 16 == lax.broadcasted_iota(
        jnp.int32, (16, span), 0
    )
    me = me_ref[0]
    full = []
    for c in range(2):
        parts = []
        for owner in range(owners):
            away = lax.rem(me - owner + owners, owners)
            piece = coeff_refs[0][0, c]
            for s in range(1, owners):
                piece = jnp.where(away == s, coeff_refs[s][0, c], piece)
            parts.append(piece)
        full.append(jnp.concatenate(parts, 0))
    lines = [[], []]
    for kb in range(per_chunk):
        w = panels_ref[:, kb * 16 : (kb + 1) * 16, :].reshape(span, DEG)
        both = jnp.concatenate([full[c][kb * 16 : (kb + 1) * 16] for c in range(2)], 0)
        o = lax.dot_general(both, w, (((1,), (1,)), ((), ())), preferred_element_type=f32)
        for c in range(2):
            kept = jnp.where(mask, o[16 * c : 16 * c + 16], 0.0)
            lines[c].append(jnp.sum(kept, axis=0, keepdims=True))
    block = jnp.concatenate(lines[0] + lines[1], 0).astype(out_ref.dtype)
    for d in range(dests):
        out_ref[d, 0] = block[:, d * wide : (d + 1) * wide]


def synthesis(me, pieces, panels, dests, wide):
    chunks, _, size, _ = pieces[0].shape
    chunk = size * len(pieces)
    per_chunk = chunk // 16
    piece_spec = pl.BlockSpec((1, 2, size, DEG), lambda i: (i, 0, 0, 0))
    return pl.pallas_call(
        functools.partial(synthesis_kernel, per_chunk),
        grid=(chunks,),
        in_specs=[pl.BlockSpec(memory_space=pltpu.SMEM)]
        + [piece_spec] * len(pieces)
        + [pl.BlockSpec((panels.shape[0], chunk, DEG), lambda i: (0, i, 0))],
        out_specs=pl.BlockSpec((dests, 1, 2 * per_chunk, wide), lambda i: (0, i, 0, 0)),
        out_shape=jax.ShapeDtypeStruct((dests, chunks, 2 * per_chunk, wide), bf16),
        name="synthesis",
    )(me, *pieces, panels)


def inverse_kernel(
    per_chunk, chunks, addr_ref, s_ref, first_ref, twist_ref, last_ref, out_ref, table, g, va, vb
):
    cycles = out_ref.shape[0]
    table[...] = jnp.zeros(table.shape, f32)
    g[...] = jnp.zeros(g.shape, f32)

    def place(b, carry):
        for n in range(BATCH):
            rows = []
            for c in range(2):
                for h in range(2):
                    for u in range(8 // per_chunk):
                        piece = (b * BATCH + n) * (8 // per_chunk) + u
                        block = s_ref[piece // chunks, piece % chunks].astype(f32)
                        rows.append(
                            block[c * per_chunk : (c + 1) * per_chunk, h * 128 : (h + 1) * 128]
                        )
            turned = swap_blocks(jnp.concatenate(rows, 0))
            g[128 * n : 128 * n + 128, : 2 * cycles] = turned.T
        for i in range(128 * BATCH):
            table[pl.ds(addr_ref[b * 128 * BATCH + i], 1), :] = g[pl.ds(i, 1), :]
        return carry

    lax.fori_loop(0, ORDERS // 128 // BATCH, place, 0)

    def first_stage(pair, carry):
        total = None
        for e in range(2):
            base = pl.multiple_of((2 * pair + e) * 64, 64)
            plus = table[pl.ds(base, QPAD), :]
            minus = table[pl.ds(base + QPAD, QPAD), :]
            both = plus + minus
            if e:
                both = pltpu.roll(both, 64, 1)
            both = both + pltpu.roll(plus - minus, 64 * e + 32, 1)
            total = both if total is None else total + both
        high = total.astype(bf16).astype(f32)
        stacked = jnp.concatenate([high, total - high, high], 0).T.astype(bf16)
        x = jnp.dot(stacked, first_ref[...], preferred_element_type=f32)
        for e in range(2):
            k = 2 * pair + e
            p_re, p_im, m_re, m_im = (
                x[64 * e + 16 * i : 64 * e + 16 * i + 16] for i in range(4)
            )
            t_re = p_re[:, :LANES] - p_im[:, LANES:]
            t_im = m_re[:, LANES:] + m_im[:, :LANES]
            cosine = twist_ref[0, pl.ds(k, 1), :]
            sine = twist_ref[1, pl.ds(k, 1), :]
            v_re = t_re * cosine - t_im * sine
            v_im = t_re * sine + t_im * cosine
            for row, v in ((k, v_re), (KPAD + k, v_im)):
                va[pl.ds(row, cycles, stride=IPITCH), :] = v[:, :128]
                vb[pl.ds(row, cycles, stride=IPITCH), :] = v[:, 128:]
        return carry

    lax.fori_loop(0, KPAD // 2, first_stage, 0, unroll=4)

    rest = FAST - 128

    def last_stage(r, carry):
        base = pl.multiple_of(r * IPITCH, 8)
        rows = pl.ds(base, 2 * KPAD)
        high, low = split(jnp.concatenate([va[rows, :], vb[rows, 0:rest]], 1))
        o = jnp.dot(last_ref[...], high, preferred_element_type=f32)
        o = o[:APAD] + o[APAD:]
        o = o + jnp.dot(last_ref[:APAD], low, preferred_element_type=f32)
        out_ref[r] = o[:SLOW]
        return carry

    lax.fori_loop(0, cycles, last_stage, 0)


def inverse(returned, addr, cycles, scale):
    sources, chunks, rows, wide = returned.shape
    per_chunk = rows // 2
    first, twist, last = inverse_tables(scale)
    vmem = pl.BlockSpec(memory_space=pltpu.VMEM)
    field = pl.pallas_call(
        functools.partial(inverse_kernel, per_chunk, chunks),
        in_specs=[pl.BlockSpec(memory_space=pltpu.SMEM)] + [vmem] * 4,
        out_specs=vmem,
        out_shape=jax.ShapeDtypeStruct((cycles, SLOW, FAST), f32),
        scratch_shapes=[
            pltpu.VMEM((KPAD * 64, 128), f32),
            pltpu.VMEM((128 * BATCH, 128), f32),
            pltpu.VMEM((cycles * IPITCH, 128), f32),
            pltpu.VMEM((cycles * IPITCH, 128), f32),
        ],
        name="inverse",
    )(addr, returned, first, twist, last)
    return field.reshape(cycles, LON)


def exchange(blocks, axis, count, me):
    got = []
    for s in range(1, count):
        block = lax.dynamic_index_in_dim(blocks, lax.rem(me + s, count), 0, keepdims=False)
        got.append(lax.ppermute(block, axis, [(i, (i + s) % count) for i in range(count)]))
    return got


def local(heights, panels, ord_slot, cutoffs):
    lat_count = lax.axis_size("lat")
    ord_count = lax.axis_size("ord")
    me = lax.axis_index("lat")
    cycles = heights.shape[0]
    slots = panels.shape[1]
    order = ord_slot + 1
    rest = order % SLOW
    turn = order // SLOW
    addr = jnp.where(
        rest < HALF, rest * 64 + turn, (SLOW - rest) * 64 + QPAD + turn + 1
    ).astype(jnp.int32)

    picked = forward(heights, addr, ord_count, slots)
    picked = lax.all_to_all(picked, "ord", split_axis=0, concat_axis=0, tiled=True)

    stride = (NMAX - ORDERS) // DEG
    degree_int = ORDERS + np.arange(DEG, dtype=np.int32) * stride
    degree = degree_int.astype(np.float32)
    factors = np.zeros((8, DEG), np.float32)
    factors[0] = 1.0
    factors[1] = (degree + 2.0) / (2.0 * NMAX)
    factors[2] = (degree + 2.0) * (degree + 1.0) / (6.0 * NMAX * NMAX)
    terms = analysis(picked, panels, jnp.asarray(factors), lat_count)

    mine = lax.dynamic_index_in_dim(terms, me, 0, keepdims=False).astype(f32)
    for other in exchange(terms, "lat", lat_count, me):
        mine = mine + other.astype(f32)
    chunks, _, size, _ = mine.shape
    limits = lax.dynamic_index_in_dim(
        cutoffs.reshape(chunks, lat_count, size), me, 1, keepdims=False
    )
    keep = jnp.asarray(degree_int)[None, None, :] <= limits[:, :, None]
    coeffs = jnp.where(keep[:, None], mine, 0.0).astype(bf16)
    pieces = [coeffs]
    for s in range(1, lat_count):
        pairs = [(i, (i + s) % lat_count) for i in range(lat_count)]
        pieces.append(lax.ppermute(coeffs, "lat", pairs))

    back = synthesis(me.astype(jnp.int32).reshape(1), pieces, panels, ord_count, 16 * cycles)
    back = lax.all_to_all(back, "ord", split_axis=0, concat_axis=0, tiled=True)
    cycles_all = cycles * lat_count * ord_count
    return inverse(back, addr, cycles, math.sqrt(cycles_all / (DEG * ORDERS)))


def solution(mesh):
    return jax.shard_map(
        local,
        mesh=mesh,
        in_specs=(P(("lat", "ord"), None), P("lat", "ord", None), P(), P("ord")),
        out_specs=P(("lat", "ord"), None),
        check_vma=False,
    )
```

time: 493 us -> 144 us (0.29); the launches traced: 486 us -> 142 us
  matrix products: 172 us -> 0 us
  local copies, waits for them, and re-layouts: 145 us -> 11.1 us
  other arithmetic: 73.1 us -> 2.39 us
  Pallas kernels: 0 us -> 67.1 us
  waiting for transfers between devices: 70.1 us -> 31 us
  blocking collectives: 0 us -> 18.1 us
  between operations: 14 us -> 0.08 us
    dot_general x8 -> x0, matrix products: 172 us -> none  [the longest x1 50.4 us: local(): jnp.einsum('rkn,ckn->crk', panels, coeffs, preferred_element_type=jnp.flo...]
    pallas_call x0 -> x4, Pallas kernels: none -> 67.1 us  [the longest x1 24.2 us: forward(): pl.pallas_call(functools.partial(forward_kernel, per_chunk, chunks), in_s...]
    psum x1 -> x0, waiting for transfers between devices: 45.9 us -> none  [local(): total = lax.psum(terms, 'lat')]
    gather x2 -> x0, local copies, waits for them, and re-layouts: 30.2 us -> none  [the longest x1 15.1 us: local(): spec_real[:, ord_slot].reshape(3, cycle_dev, ORDERS)]
    scatter x4 -> x0, local copies, waits for them, and re-layouts: 29.5 us -> none  [local(): jnp.zeros((cycle_dev, blocks * LON_SLOW), jnp.float32).at[:, target]]
    sin x1 -> x0, other arithmetic: 26.6 us -> none  [twiddle_tables(): return (jnp.cos(angle), jnp.sin(angle))]
    neg x1 -> x0, other arithmetic: 26.4 us -> none  [forward_spectra(): -twist_sin]
    unnamed x12 -> x15, local copies, waits for them, and re-layouts: 22.5 us -> 1.58 us
  transfers between devices with their start and end apart: 3 -> 7, of which waited for: 2 -> 7; matrix products, arithmetic and copies ran while one was open for 6% -> 0% of each run, Pallas kernels for 0% -> 0%
where the time goes in v1:
time: 144 us; the launch traced here: 142 us
  Pallas kernels  67.1 us (47%)
  waiting for transfers between devices  31 us (22%)
  blocking collectives  18.1 us (13%)
  starting transfers between devices  12.6 us (9%)
  local copies, waits for them, and re-layouts  11.1 us (8%)
  other arithmetic  2.39 us (2%)
    pallas_call x1, Pallas kernels, forward(): pl.pallas_call(functools.partial(forward_kernel, per_chunk, chunks), in_s...  24.2 us
    all_to_all x1, waiting for transfers between devices, local(): lax.all_to_all(picked, 'ord', split_axis=0, concat_axis=0, tiled=True)  24.1 us
    pallas_call x1, Pallas kernels, inverse(): pl.pallas_call(functools.partial(inverse_kernel, per_chunk, chunks), in_s...  19.9 us
    all_to_all x1, blocking collectives, local(): back = lax.all_to_all(back, 'ord', split_axis=0, concat_axis=0, tiled=True)  18.1 us
    pallas_call x1, Pallas kernels, synthesis(): pl.pallas_call(functools.partial(synthesis_kernel, per_chunk), grid=(chun...  12.2 us
    pallas_call x1, Pallas kernels, analysis(): pl.pallas_call(functools.partial(analysis_kernel, per_chunk), grid=(chunk...  10.8 us
    all_to_all x1, starting transfers between devices, local(): lax.all_to_all(picked, 'ord', split_axis=0, concat_axis=0, tiled=True)  6.41 us
    reshape x1, local copies, waits for them, and re-layouts, forward(): heights.reshape(cycles, SLOW, FAST)  4.56 us
  transfers between devices with their start and end apart: 7, of which 7 were waited for; matrix products, arithmetic and copies ran while one was open for 0% of the time, Pallas kernels for 0%

profile of v1, /device:TPU:1, one launch (start us, length us, event | category | flops | bytes accessed | tf_op | source)
XLA Modules:
  0.0 142.3 jit_solution(15516184761173165220)
XLA Ops:
  0.0 1.4 add_select_fusion.2.addr_ref
  1.4 4.6 %reshape.20.x_ref = bf16[16,180,240]{2,1,0:T(8,128)(2,1)} reshape(bf16[16,43200]{1,0:T(8,128)(2,1)} %param.12) | data formatting | bytes 2764800 | tf_op jit(solution)/shard_map/reshape | solution.py:178
  5.9 24.2 %forward.1 = bf16[8,5,48,256]{3,2,1,0:T(8,128)(2,1)} custom-call(s32[5120]{0:T(1024)} %add_select_fusion.2.addr_ref, bf16[16,180,240]{2,1,0:T(8,128)(2,1)} %reshape.20.x_ref, bf16[384,180]{1,0:T(8,128)(2,1)} %constant.78.clone.first_ref, f32[2,96,240]{2,1,0:T(8,128)} %constant.79.clone.twist_ref, bf16[128,240]{1,0:T(8,128)(2,1)} %constant.80.clone.last_ref), custom_call_target="tpu_custom_call" | custom-call | tf_op jit(solution)/shard_map/forward/pallas_call | solution.py:166
  30.2 6.4 %all-to-all-start = ((bf16[8,5,48,256]{3,2,1,0:T(8,128)(2,1)}), bf16[8,5,48,256]{3,2,1,0:T(8,128)(2,1)S(1)}, u32[]{:S(2)}, u32[]{:S(2)}) async-start(bf16[8,5,48,256]{3,2,1,0:T(8,128)(2,1)} %forward.1), calls=%async_computation | async-start | bytes 1966080 | tf_op jit(solution)/shard_map/all_to_all | solution.py:400
  36.6 0.0 copy-done.5
  36.6 0.1 reshape.19
  36.7 0.0 copy-start.6
  36.7 24.1 %all-to-all-done.p_ref = bf16[8,5,48,256]{3,2,1,0:T(8,128)(2,1)S(1)} async-done(((bf16[8,5,48,256]{3,2,1,0:T(8,128)(2,1)}), bf16[8,5,48,256]{3,2,1,0:T(8,128)(2,1)S(1)}, u32[]{:S(2)}, u32[]{:S(2)}) %all-to-all-start) | async-done | bytes 983072 | tf_op jit(solution)/shard_map/all_to_all | solution.py:400
  60.8 0.9 copy-done
  61.7 10.8 %analysis.1 = bf16[4,5,2,32,128]{4,3,2,1,0:T(8,128)(2,1)} custom-call(bf16[8,5,48,256]{3,2,1,0:T(8,128)(2,1)} %copy-done, bf16[128,640,128]{2,1,0:T(8,128)(2,1)} %refs_4_.1, f32[8,128]{1,0:T(8,128)} %constant.81.clone.q_ref), custom_call_target="tpu_custom_call" | custom-call | tf_op jit(solution)/shard_map/analysis/pallas_call | solution.py:220
  72.5 1.0 dynamic-slice_bitcast_fusion.2
  73.4 1.2 collective-permute-start
  74.7 1.2 collective-permute-start.2
  75.9 1.2 collective-permute-start.1
  77.1 0.0 copy-done.6
  77.1 0.1 broadcast_compare_fusion
  77.2 0.5 collective-permute-done
  77.7 1.6 %collective-permute-done.2 = bf16[5,2,32,128]{3,2,1,0:T(8,128)(2,1)S(1)} collective-permute-done((bf16[5,2,32,128]{3,2,1,0:T(8,128)(2,1)S(1)}, bf16[5,2,32,128]{3,2,1,0:T(8,128)(2,1)S(1)}, u32[]{:S(2)}, u32[]{:S(2)}) %collective-permute-start.2) | collective-permute-done | bytes 81952 | tf_op jit(solution)/shard_map/ppermute | solution.py:382
  79.2 1.1 collective-permute-done.1
  80.3 0.9 fusion.3.refs_0_
  81.3 0.0 copy-start.1
  81.3 1.0 collective-permute-start.5
  82.3 0.6 collective-permute-start.4
  82.9 0.8 collective-permute-start.3
  83.7 0.9 collective-permute-done.5.refs_3_
  84.6 1.0 collective-permute-done.4.refs_2_
  85.6 2.0 %collective-permute-done.3.refs_1_ = bf16[5,2,32,128]{3,2,1,0:T(8,128)(2,1)S(1)} collective-permute-done((bf16[5,2,32,128]{3,2,1,0:T(8,128)(2,1)S(1)}, bf16[5,2,32,128]{3,2,1,0:T(8,128)(2,1)S(1)}, u32[]{:S(2)}, u32[]{:S(2)}) %collective-permute-start.3) | collective-permute-done | bytes 81952 | tf_op jit(solution)/shard_map/ppermute | solution.py:423
  87.6 0.6 copy-done.4
  88.2 12.2 %synthesis.1 = bf16[8,5,16,256]{3,2,1,0:T(8,128)(2,1)} custom-call(s32[1]{0:T(128)} %bitcast.me_ref, bf16[5,2,32,128]{3,2,1,0:T(8,128)(2,1)} %copy-done.1, bf16[5,2,32,128]{3,2,1,0:T(8,128)(2,1)} %copy-done.4, bf16[5,2,32,128]{3,2,1,0:T(8,128)(2,1)} %copy-done.3, bf16[5,2,32,128]{3,2,1,0:T(8,128)(2,1)} %copy-done.2, bf16[128,640,128]{2,1,0:T(8,128)(2,1)} %refs_4_.1), custom_call_target="tpu_custom_call" | custom-call | tf_op jit(solution)/shard_map/synthesis/pallas_call | solution.py:272
  100.4 18.1 %all_to_all.10.s_ref = bf16[8,5,16,256]{3,2,1,0:T(8,128)(2,1)} all-to-all(bf16[8,5,16,256]{3,2,1,0:T(8,128)(2,1)} %synthesis.1), channel_id=1, replica_groups=mesh['lat'=4,'ord'=8] {'ord'}, dimensions={0} | all-to-all | bytes 655360 | tf_op jit(solution)/shard_map/all_to_all | solution.py:426
  118.5 19.9 %inverse.1 = f32[16,180,240]{2,1,0:T(8,128)} custom-call(s32[5120]{0:T(1024)} %add_select_fusion.2.addr_ref, bf16[8,5,16,256]{3,2,1,0:T(8,128)(2,1)} %all_to_all.10.s_ref, bf16[96,512]{1,0:T(8,128)(2,1)} %constant.83.clone.first_ref, f32[2,96,256]{2,1,0:T(8,128)} %constant.84.clone.twist_ref, bf16[368,192]{1,0:T(8,128)(2,1)} %constant.85.clone.last_ref), custom_call_target="tpu_custom_call" | custom-call | tf_op jit(solution)/shard_map/inverse/pallas_call | solution.py:362
  138.4 3.9 %reshape.21 = f32[16,43200]{1,0:T(8,128)} reshape(f32[16,180,240]{2,1,0:T(8,128)} %inverse.1) | data formatting | bytes 5529600 | tf_op jit(solution)/shard_map/reshape | solution.py:375
  (10 shorter events, 0.0 us)
Async XLA Ops:
  5.9 30.6 %copy-start.5 = (s32[640]{0:T(1024)S(1)}, s32[640]{0:T(1024)}, u32[]{:S(2)}) copy-start(s32[640]{0:T(1024)} %param.15) | copy-start | bytes 7684
  30.2 30.6 %all-to-all-start = ((bf16[8,5,48,256]{3,2,1,0:T(8,128)(2,1)}), bf16[8,5,48,256]{3,2,1,0:T(8,128)(2,1)S(1)}, u32[]{:S(2)}, u32[]{:S(2)}) async-start(bf16[8,5,48,256]{3,2,1,0:T(8,128)(2,1)} %forward.1), calls=%async_computation | async-start | bytes 1966080 | tf_op jit(solution)/shard_map/all_to_all | solution.py:400
  36.7 40.4 %copy-start.6 = (s32[128]{0:T(128)S(1)}, s32[128]{0:T(128)}, u32[]{:S(2)}) copy-start(s32[128]{0:T(128)} %constant.82.clone) | copy-start | bytes 1540
  60.8 0.9 copy-start
  73.4 4.2 %collective-permute-start = (bf16[5,2,32,128]{3,2,1,0:T(8,128)(2,1)S(1)}, bf16[5,2,32,128]{3,2,1,0:T(8,128)(2,1)S(1)}, u32[]{:S(2)}, u32[]{:S(2)}) collective-permute-start(bf16[5,2,32,128]{3,2,1,0:T(8,128)(2,1)S(1)} %get-tuple-element.5), channel_id=1, source_target_pairs={{0,8},{8,16},{16,24},{24,0},{1,9},{9,17},{17,25},{25,1},{2,10},{10... | collective-permute-start | bytes 245768 | tf_op jit(solution)/shard_map/ppermute | solution.py:382
  74.7 4.6 %collective-permute-start.2 = (bf16[5,2,32,128]{3,2,1,0:T(8,128)(2,1)S(1)}, bf16[5,2,32,128]{3,2,1,0:T(8,128)(2,1)S(1)}, u32[]{:S(2)}, u32[]{:S(2)}) collective-permute-start(bf16[5,2,32,128]{3,2,1,0:T(8,128)(2,1)S(1)} %get-tuple-element.6), channel_id=1, source_target_pairs={{0,24},{8,0},{16,8},{24,16},{1,25},{9,1},{17,9},{25,17},{2,26},{10... | collective-permute-start | bytes 245768 | tf_op jit(solution)/shard_map/ppermute | solution.py:382
  75.9 4.4 %collective-permute-start.1 = (bf16[5,2,32,128]{3,2,1,0:T(8,128)(2,1)S(1)}, bf16[5,2,32,128]{3,2,1,0:T(8,128)(2,1)S(1)}, u32[]{:S(2)}, u32[]{:S(2)}) collective-permute-start(bf16[5,2,32,128]{3,2,1,0:T(8,128)(2,1)S(1)} %get-tuple-element.7), channel_id=1, source_target_pairs={{0,16},{8,24},{16,0},{24,8},{1,17},{9,25},{17,1},{25,9},{2,18},{10... | collective-permute-start | bytes 245768 | tf_op jit(solution)/shard_map/ppermute | solution.py:382
  81.3 6.3 %copy-start.1 = (bf16[5,2,32,128]{3,2,1,0:T(8,128)(2,1)}, bf16[5,2,32,128]{3,2,1,0:T(8,128)(2,1)S(1)}, u32[]{:S(2)}) copy-start(bf16[5,2,32,128]{3,2,1,0:T(8,128)(2,1)S(1)} %fusion.3.refs_0_) | copy-start | bytes 245764
  81.3 3.3 %collective-permute-start.5 = (bf16[5,2,32,128]{3,2,1,0:T(8,128)(2,1)S(1)}, bf16[5,2,32,128]{3,2,1,0:T(8,128)(2,1)S(1)}, u32[]{:S(2)}, u32[]{:S(2)}) collective-permute-start(bf16[5,2,32,128]{3,2,1,0:T(8,128)(2,1)S(1)} %fusion.3.refs_0_), channel_id=1, source_target_pairs={{0,24},{8,0},{16,8},{24,16},{1,25},{9,1},{17,9},{25,17},{2,26},{10... | collective-permute-start | bytes 245768 | tf_op jit(solution)/shard_map/ppermute | solution.py:423
  82.3 3.3 %collective-permute-start.4 = (bf16[5,2,32,128]{3,2,1,0:T(8,128)(2,1)S(1)}, bf16[5,2,32,128]{3,2,1,0:T(8,128)(2,1)S(1)}, u32[]{:S(2)}, u32[]{:S(2)}) collective-permute-start(bf16[5,2,32,128]{3,2,1,0:T(8,128)(2,1)S(1)} %fusion.3.refs_0_), channel_id=1, source_target_pairs={{0,16},{8,24},{16,0},{24,8},{1,17},{9,25},{17,1},{25,9},{2,18},{10... | collective-permute-start | bytes 245768 | tf_op jit(solution)/shard_map/ppermute | solution.py:423
  82.9 4.6 %collective-permute-start.3 = (bf16[5,2,32,128]{3,2,1,0:T(8,128)(2,1)S(1)}, bf16[5,2,32,128]{3,2,1,0:T(8,128)(2,1)S(1)}, u32[]{:S(2)}, u32[]{:S(2)}) collective-permute-start(bf16[5,2,32,128]{3,2,1,0:T(8,128)(2,1)S(1)} %fusion.3.refs_0_), channel_id=1, source_target_pairs={{0,8},{8,16},{16,24},{24,0},{1,9},{9,17},{17,25},{25,1},{2,10},{10... | collective-permute-start | bytes 245768 | tf_op jit(solution)/shard_map/ppermute | solution.py:423
  84.6 2.9 %copy-start.2 = (bf16[5,2,32,128]{3,2,1,0:T(8,128)(2,1)}, bf16[5,2,32,128]{3,2,1,0:T(8,128)(2,1)S(1)}, u32[]{:S(2)}) copy-start(bf16[5,2,32,128]{3,2,1,0:T(8,128)(2,1)S(1)} %collective-permute-done.5.refs_3_) | copy-start | bytes 245764
  85.6 2.0 %copy-start.3 = (bf16[5,2,32,128]{3,2,1,0:T(8,128)(2,1)}, bf16[5,2,32,128]{3,2,1,0:T(8,128)(2,1)S(1)}, u32[]{:S(2)}) copy-start(bf16[5,2,32,128]{3,2,1,0:T(8,128)(2,1)S(1)} %collective-permute-done.4.refs_2_) | copy-start | bytes 245764
  87.5 0.6 copy-start.4
